TPU v7x, 32 devices: a whole 2x2x4 slice. The times are simulated.
32 devices in a mesh: seq: 16 (over z, x, core), head: 2 (over y).
Axes of the slice: x: 2, y: 2, z: 4, core: 2. Of those that a mesh axis runs over, the one named last changes fastest.
Arguments:
- sparse_query: bfloat16 [4096, 8192], P('seq', 'head'), may hold values from -62 to 62
- sparse_key: bfloat16 [4096, 1024], P('seq', 'head'), may hold values from -5 to 5
- sparse_value: bfloat16 [4096, 1024], P('seq', 'head'), may hold values from -5 to 5
- light_query: bfloat16 [4096, 8192], P('seq', 'head'), may hold values from -60 to 60
- light_key: bfloat16 [4096, 8192], P('seq', 'head'), may hold values from -0.5 to 0.5
- log_decay: float32 [64, 4096], P('head', 'seq'), may hold values from -1 to 0
- segments: int32 [4096], P('seq'), may hold values from 0 to 3, never falling along the last dimension, each value on 1 to 2048 neighbouring positions
- block_list: int32 [32, 12], P('seq'), may hold values from -1 to 29, as said below
Outputs:
- sparse_out: bfloat16 [4096, 8192], P('seq', 'head')
- mixed_out: bfloat16 [4096, 8192], P('seq', 'head')
Inputs may be any that keep to these rules, and one draw needn't show every extreme that they name: `block_list`: entry -1 names no block. Every other entry of row b names a block of an earlier aligned group of 256 tokens than the group that holds block b; the rows of one aligned group of 256 tokens together name at most one block of any other group, and name it at most once. Some row names 12 blocks. `segments`: document ids may be packed several to a wider word wherever they travel.
All inputs are finite; a program needn't handle non-finite values.
Results may differ from a plain program's by a relative error of at most 0.0057.
Values may be sent and summed in bfloat16 or wider, within the bound.
No kernel may reach another device: no remote copies, remote signals or barrier semaphores. Data moves between devices by JAX's collectives and lax.ppermute only.
A program may use at most 128 MiB of HBM per device.

v0:
```python
import jax
import jax.numpy as jnp
from jax import lax
from jax.sharding import PartitionSpec as P

ASKER_CHANNELS = 64
HD = 128
BLK = 128
big_negative = -1e30
norm_eps = 1e-06


def passed_along(value, axis, by):
    size = lax.axis_size(axis)
    pairs = [(i, i + by) for i in range(size) if 0 <= i + by < size]
    return lax.ppermute(value, axis, pairs)


def carried_in(value, axis, join, neutral):
    count, mine = (lax.axis_size(axis), lax.axis_index(axis))
    pieces = jax.tree.map(lambda part: lax.all_gather(part, axis), value)
    subtotal = jax.tree.map(
        lambda part, zero: jnp.full_like(part, 0) + jnp.asarray(zero, part.dtype), value, neutral
    )

    def turn(position, subtotal):
        longer = join(subtotal, jax.tree.map(lambda part: part[position], pieces))
        return jax.tree.map(lambda new, old: jnp.where(position < mine, new, old), longer, subtotal)

    return lax.fori_loop(0, count - 1, turn, subtotal)


def attend_block(query, own_kv, own_seg, picked_kv, picked_seg, picked_ok):
    row_count = query.shape[0]
    kv_width = own_kv.shape[1] // 2
    kv_heads = kv_width // HD
    group_size = query.shape[1] // kv_width
    list_count = picked_kv.shape[0]
    keys_all = jnp.concatenate(
        [own_kv, picked_kv.reshape(list_count * row_count, 2 * kv_width)], axis=0
    )
    seg_all = jnp.concatenate([own_seg, picked_seg.reshape(list_count * row_count)])
    queries = query.reshape(row_count, kv_heads, group_size, HD)
    key_part = keys_all[:, :kv_width].reshape(-1, kv_heads, HD)
    value_part = keys_all[:, kv_width:].reshape(-1, kv_heads, HD)
    scores = jnp.einsum(
        "qkgd,nkd->kgqn", queries, key_part, preferred_element_type=jnp.float32
    ) * HD ** (-0.5)
    places = jnp.arange(row_count)
    causal = places[None, :] <= places[:, None]
    listed_ok = jnp.broadcast_to(
        jnp.repeat(picked_ok, row_count)[None, :], (row_count, list_count * row_count)
    )
    allowed = jnp.concatenate([causal, listed_ok], axis=1) & (seg_all[None, :] == own_seg[:, None])
    scores = jnp.where(allowed[None, None], scores, big_negative)
    highest = jnp.max(scores, axis=-1, keepdims=True)
    lifted = jnp.exp(scores - highest)
    weights = (lifted / jnp.sum(lifted, axis=-1, keepdims=True)).astype(jnp.bfloat16)
    result = jnp.einsum("kgqn,nkd->qkgd", weights, value_part, preferred_element_type=jnp.float32)
    return result.astype(jnp.bfloat16).reshape(row_count, kv_heads * group_size * HD)


def light_local(queries, keyed, valued, rates, doc_ids, prior_doc):
    running = jnp.cumsum(rates, axis=1)
    block_total = running[:, -1]
    places = jnp.arange(doc_ids.shape[0])
    spread = running[:, :, None] - running[:, None, :]
    visible = (places[None, :] <= places[:, None]) & (doc_ids[None, :] == doc_ids[:, None])
    decay_mask = jnp.where(visible[None], jnp.exp(jnp.minimum(spread, 0.0)), 0.0)
    scores = jnp.einsum("thd,shd->hts", queries, keyed, preferred_element_type=jnp.float32)
    weights = (scores * decay_mask).astype(jnp.bfloat16)
    inside = jnp.einsum("hts,shd->thd", weights, valued, preferred_element_type=jnp.float32)
    reach_factor = jnp.exp(running) * (doc_ids == prior_doc).astype(jnp.float32)[None, :]
    fading = (
        jnp.exp(block_total[:, None] - running)
        * (doc_ids == doc_ids[-1]).astype(jnp.float32)[None, :]
    )
    scaled = keyed.astype(jnp.float32) * jnp.transpose(fading)[:, :, None]
    added_state = jnp.einsum(
        "shd,she->hde", scaled, valued.astype(jnp.float32), precision=lax.Precision.HIGHEST
    )
    carry_factor = jnp.exp(block_total) * (doc_ids[-1] == prior_doc).astype(jnp.float32)
    return (inside, reach_factor, added_state, carry_factor)


def chain_link(earlier, latter):
    return (earlier[0] * latter[0], latter[0][:, None, None] * earlier[1] + latter[1])


def body(
    sparse_query, sparse_key, sparse_value, light_query, light_key, log_decay, segments, block_list
):
    tokens_here = sparse_query.shape[0]
    block_count = tokens_here // BLK
    kv_width = sparse_key.shape[1]
    shard_count = lax.axis_size("seq")
    kv_local = jnp.concatenate([sparse_key, sparse_value], axis=1)
    local_blocks = kv_local.reshape(block_count, BLK, 2 * kv_width)
    seg_blocks = segments.reshape(block_count, BLK)
    owner_index = jnp.where(block_list >= 0, block_list // block_count, -1).reshape(-1)
    inner_index = (block_list % block_count).reshape(-1)
    owner_match = jnp.arange(shard_count)[:, None] == owner_index[None, :]
    wanted = jnp.max(jnp.where(owner_match, inner_index[None, :], -1), axis=1)
    wanted_safe = jnp.clip(wanted, 0, block_count - 1)
    owner_table = owner_index.reshape(block_count, block_list.shape[1])
    kv_portion = lax.all_gather(kv_local, "seq", axis=0, tiled=True)
    seg_portion = lax.all_gather(segments, "seq", axis=0, tiled=True)
    portion_shards = kv_portion.shape[0] // tokens_here
    kv_view = kv_portion.reshape(portion_shards, block_count, BLK, 2 * kv_width)
    seg_view = seg_portion.reshape(portion_shards, block_count, BLK)
    pick_block = wanted_safe[:, None] == jnp.arange(block_count)[None, :]
    owners_here = jnp.arange(portion_shards)
    owner_hit = owner_table[:, :, None] == owners_here[None, None, :]
    selector = owner_hit[:, :, :, None] & pick_block[None, None, :, :]
    new_kv = jnp.einsum(
        "bkpj,pjnc->bknc",
        selector.astype(jnp.bfloat16),
        kv_view,
        preferred_element_type=jnp.float32,
    )
    new_seg = jnp.sum(jnp.where(selector[:, :, :, :, None], seg_view[None, None], 0), axis=(2, 3))
    picked_kv = new_kv.astype(jnp.bfloat16)
    picked_seg = new_seg.astype(jnp.int32)
    picked_ok = block_list >= 0
    query_blocks = sparse_query.reshape(block_count, BLK, sparse_query.shape[1])
    sparse_out = jnp.concatenate(
        [
            attend_block(
                query_blocks[block_index],
                local_blocks[block_index],
                seg_blocks[block_index],
                picked_kv[block_index],
                picked_seg[block_index],
                picked_ok[block_index],
            )
            for block_index in range(block_count)
        ],
        axis=0,
    )
    heads_here = light_query.shape[1] // HD
    light_q = light_query.reshape(block_count, BLK, heads_here, HD)
    light_k = light_key.reshape(block_count, BLK, heads_here, HD)
    light_v = sparse_out.reshape(block_count, BLK, heads_here, HD)
    rate_blocks = log_decay.reshape(heads_here, block_count, BLK)
    before = passed_along(segments[tokens_here - 1 :] + 1, "seq", 1) - 1
    block_parts = []
    for block_index in range(block_count):
        prior_doc = before[0] if block_index == 0 else seg_blocks[block_index - 1, BLK - 1]
        block_parts.append(
            light_local(
                light_q[block_index],
                light_k[block_index],
                light_v[block_index],
                rate_blocks[:, block_index],
                seg_blocks[block_index],
                prior_doc,
            )
        )
    carried = jnp.zeros((heads_here, HD, HD), jnp.float32)
    passed = jnp.ones((heads_here,), jnp.float32)
    for block_item in block_parts:
        carried = block_item[3][:, None, None] * carried + block_item[2]
        passed = passed * block_item[3]
    entering = carried_in(
        (passed, carried), "seq", chain_link, (jnp.ones_like(passed), jnp.zeros_like(carried))
    )[1]
    outputs = []
    for block_index in range(block_count):
        inside, reach_factor, added_state, carry_factor = block_parts[block_index]
        outside = (
            jnp.einsum(
                "thd,hde->the",
                light_q[block_index].astype(jnp.float32),
                entering,
                precision=lax.Precision.HIGHEST,
            )
            * jnp.transpose(reach_factor)[:, :, None]
        )
        outputs.append(inside + outside)
        entering = carry_factor[:, None, None] * entering + added_state
    mixed_out = jnp.concatenate(outputs, axis=0).reshape(tokens_here, heads_here * HD)
    squares = lax.psum(jnp.sum(mixed_out * mixed_out, axis=1), "head")
    norm_scale = lax.rsqrt(squares / (ASKER_CHANNELS * HD) + norm_eps)
    return (sparse_out, (mixed_out * norm_scale[:, None]).astype(jnp.bfloat16))


def solution(mesh):
    in_specs = (
        P("seq", "head"),
        P("seq", "head"),
        P("seq", "head"),
        P("seq", "head"),
        P("seq", "head"),
        P("head", "seq"),
        P("seq"),
        P("seq", None),
    )
    out_specs = (P("seq", "head"), P("seq", "head"))
    return jax.shard_map(body, mesh=mesh, in_specs=in_specs, out_specs=out_specs, check_vma=False)
```

profile of v0, /device:TPU:0, one launch (start us, length us, event | category | flops | bytes accessed | tf_op | source)
XLA Modules:
  0.0 446.0 jit_solution(10736285755465180232)
XLA Ops:
  12.0 3.3 collective-permute-start
  16.4 23.1 %all-gather.2 = s32[16,1,256]{2,1,0:T(1,128)S(1)} all-gather(s32[1,1,256]{2,1,0:T(1,128)} %bitcast.191), channel_id=1, replica_groups=mesh['seq'=16,'head'=2] {'seq'}, dimensions={0}, use_global_device_ids=true | all-gather | bytes 17408 | tf_op jit(solution)/shard_map/all_gather | solution.py:107
  59.7 28.8 %all-gather.6.cloned.1.call-done = bf16[4096,1024]{1,0:T(8,128)(2,1)} async-done(((bf16[256,1024]{1,0:T(8,128)(2,1)}), bf16[4096,1024]{1,0:T(8,128)(2,1)}) %all-gather.6.cloned.1.call-update) | async-done | bytes 8388624 | tf_op jit(solution)/shard_map/all_gather | solution.py:106
  88.4 14.6 %bitcast_convert_fusion = bf16[2,12,128,1024]{3,1,2,0:T(8,128)(2,1)S(1)} fusion(bf16[16,2,128,1024]{3,2,1,0:T(8,128)(2,1)} %bitcast.162, pred[16,2]{0,1:T(4,128)(4,1)S(1)} %iota_compare_fusion.3, pred[2,12,16]{2,1,0:T(8,128)(4,1)S(1)} %iota_compare_fusion.1), kind=kOutput, calls=%fused_computation.13 | convolution fusion | flops 204473088 | bytes 14680480 | tf_op jit(solution)/shard_map/bkpj,pjnc->bknc/dot_general | solution.py:115
  107.9 2.9 pad_maximum_fusion.2
  110.8 3.7 copy.140
  114.5 14.5 %fusion.85 = f32[4,1664,128,8]{2,1,3,0:T(8,128)} fusion(bf16[1664,4,128,1]{0,2,3,1:T(8,128)(2,1)} %bitcast.165, bf16[128,4,8,128]{0,3,2,1:T(8,128)(2,1)} %bitcast.167), kind=kOutput, calls=%fused_computation.142 | convolution fusion | flops 1744830464 | bytes 30015488 | tf_op jit(solution)/shard_map/qkgd,nkd->kgqn/dot_general | solution.py:46
  129.0 11.3 %fusion.84 = f32[4,8,128]{2,1,0:T(8,128)S(1)} fusion(pred[128,1664]{0,1:T(8,128)(4,1)} %get-tuple-element.160, bf16[1664,4,128,1]{0,2,3,1:T(8,128)(2,1)} %bitcast.166, bf16[128,4,8,128]{0,3,2,1:T(8,128)(2,1)} %bitcast.168), kind=kOutput, calls=%fused_computation.141 | convolution fusion | flops 1772095104 | bytes 2981888 | tf_op jit(solution)/shard_map/sub | solution.py:57
  140.3 3.6 copy.137
  146.2 14.6 %fusion.86 = f32[4,1664,128,8]{2,1,3,0:T(8,128)} fusion(bf16[1664,4,128,1]{0,2,3,1:T(8,128)(2,1)} %bitcast.163, bf16[128,4,8,128]{0,3,2,1:T(8,128)(2,1)} %bitcast.169), kind=kOutput, calls=%fused_computation.143 | convolution fusion | flops 1744830464 | bytes 30015488 | tf_op jit(solution)/shard_map/qkgd,nkd->kgqn/dot_general | solution.py:46
  160.8 10.8 %fusion.83 = f32[4,8,128]{2,1,0:T(8,128)S(1)} fusion(pred[128,1664]{0,1:T(8,128)(4,1)} %get-tuple-element.161, bf16[1664,4,128,1]{0,2,3,1:T(8,128)(2,1)S(1)} %bitcast.164, bf16[128,4,8,128]{0,3,2,1:T(8,128)(2,1)} %bitcast.170), kind=kOutput, calls=%fused_computation.140 | convolution fusion | flops 1772095104 | bytes 2981888 | tf_op jit(solution)/shard_map/sub | solution.py:57
  174.0 16.0 %fusion.41 = bf16[4,128,8,128]{3,1,2,0:T(8,128)(2,1)} fusion(bf16[1664,4,128,1]{0,2,3,1:T(8,128)(2,1)} %bitcast.186, f32[4,8,128]{2,1,0:T(8,128)S(1)} %fusion.84, f32[4,1664,128,8]{2,1,3,0:T(8,128)} %fusion.85, pred[128,1664]{0,1:T(8,128)(4,1)} %get-tuple-element.160), kind=kOutput, calls=%fused_computation.57 | convolution fusion | flops 1779439232 | bytes 30244864 | tf_op jit(solution)/shard_map/kgqn,nkd->qkgd/dot_general | solution.py:59
  190.0 3.5 fusion.31
  193.5 17.0 %fusion.40 = bf16[4,128,8,128]{3,1,2,0:T(8,128)(2,1)} fusion(bf16[1664,4,128,1]{0,2,3,1:T(8,128)(2,1)} %bitcast.187, f32[4,8,128]{2,1,0:T(8,128)S(1)} %fusion.83, f32[4,1664,128,8]{2,1,3,0:T(8,128)} %fusion.86, pred[128,1664]{0,1:T(8,128)(4,1)} %get-tuple-element.161), kind=kOutput, calls=%fused_computation.56 | convolution fusion | flops 1779439232 | bytes 30244864 | tf_op jit(solution)/shard_map/kgqn,nkd->qkgd/dot_general | solution.py:59
  210.5 4.8 %multiply_add_fusion = f32[32,128,128]{2,1,0:T(8,128)} fusion(f32[32,128,128]{2,1,0:T(8,128)S(1)} %fusion.31, bf16[128,32,128]{0,2,1:T(8,128)(2,1)} %bitcast.182, bf16[128,32,128]{0,2,1:T(8,128)(2,1)S(1)} %bitcast.178, f32[128,32]{0,1:T(8,128)S(1)} %get-tuple-element.159, f32[32]{0:T(128)S(1)} %get-tuple-element.136, f32[32]{0:T(128)S(1)} %exponential_multiply_fusion.1), kind=kOutput, calls=%fused_computation.47 | convolution fusion | flops 807927808 | bytes 6308096 | tf_op jit(solution)/shard_map/shd,she->hde/dot_general | solution.py:79
  223.1 31.9 %all-reduce = f32[512]{0:T(512)S(1)} all-reduce(f32[512]{0:T(512)S(1)} %dynamic-update-slice), channel_id=2, replica_groups=mesh['seq'=16,'head'=2] {'seq'}, use_global_device_ids=true, to_apply=%add | all-reduce | flops 512 | bytes 4096
  259.7 4.8 %fusion.42 = f32[32,128,128]{1,2,0:T(8,128)} fusion(bf16[128,32,128]{0,2,1:T(8,128)(2,1)} %bitcast.181, bf16[128,32,128]{0,2,1:T(8,128)(2,1)} %bitcast.173, bf16[128,32,128]{0,2,1:T(8,128)(2,1)} %bitcast.175, f32[32,128]{1,0:T(8,128)S(1)} %copy-done.13, pred[128,128]{1,0:T(8,128)(4,1)S(1)} %copy.158), kind=kOutput, calls=%fused_computation.58 | convolution fusion | flops 271056896 | bytes 5275648 | tf_op jit(solution)/shard_map/hts,shd->thd/dot_general | solution.py:72
  264.4 4.4 fusion.43
  268.8 3.2 pad_maximum_fusion.1
  272.0 110.3 %all-gather.8.cloned.1.call-done = f32[512,128,128]{2,1,0:T(8,128)} async-done(((f32[32,128,128]{2,1,0:T(8,128)}), f32[512,128,128]{2,1,0:T(8,128)}) %all-gather.8.cloned.1.call-update) | async-done | bytes 33554448 | tf_op jit(solution)/shard_map/all_gather | solution.py:21
  382.3 32.0 %while.14 = (s32[]{:T(128)}, f32[32,128,128]{2,1,0:T(8,128)S(1)}, s32[]{:T(128)}, f32[16,32]{1,0:T(8,128)S(1)}, f32[16,32,128,128]{3,2,1,0:T(8,128)}, /*index=5*/s32[]{:T(128)}, s32[]{:T(128)}) while((s32[]{:T(128)}, f32[32,128,128]{2,1,0:T(8,128)S(1)}, s32[]{:T(128)}, f32[16,32]{1,0:T(8,128)S(1)}, ...), condition=%wide.region_9.10_spmd.clone, body=%wide.region_8.9_spmd.clone.sunk | while | flops 2097156 | bytes 6291945 | solution.py:30
  414.3 4.0 fusion.24
  423.0 5.6 %copy.172 = f32[256,32,128]{0,2,1:T(8,128)} copy(f32[256,32,128]{2,0,1:T(8,128)} %get-tuple-element.141) | data formatting | bytes 8388608 | tf_op jit(solution)/shard_map/concatenate | solution.py:181
  428.6 4.9 %psum.7 = f32[256]{0:T(256)S(1)} all-reduce(f32[256]{0:T(256)S(1)} %get-tuple-element.140), channel_id=1, replica_groups=mesh['seq'=16,'head'=2] {'head'}, use_global_device_ids=true, to_apply=%region_11.12 | all-reduce | flops 256 | bytes 2048 | tf_op jit(solution)/shard_map/psum | solution.py:182
  (139 shorter events, 85.7 us)
Async XLA Ops:
  7.2 81.2 %all-gather.6.cloned.1.call-start = ((), (), s32[]{:S(2)}) async-start(), calls=%async_computation | async-start | bytes 8912896 | tf_op jit(solution)/shard_map/all_gather | solution.py:106
  9.2 0.8 copy-start.5
  10.0 372.3 %all-gather.8.cloned.1.call-start = ((), (), s32[]{:S(2)}) async-start(), calls=%async_computation.1 | async-start | bytes 35651584 | tf_op jit(solution)/shard_map/all_gather | solution.py:21
  12.0 43.2 %collective-permute-start = (s32[1]{0:T(128)}, s32[1]{0:T(128)}, u32[]{:S(2)}, u32[]{:S(2)}) collective-permute-start(s32[1]{0:T(128)} %add.64), channel_id=1, source_target_pairs={{0,2},{2,4},{4,6},{6,8},{8,10},{10,12},{12,14},{14,16},{16,18},{18... | collective-permute-start | bytes 20 | tf_op jit(solution)/shard_map/ppermute | solution.py:16
  42.0 1.4 copy-start.17
  42.0 3.0 copy-start.16
  45.4 13.6 %copy-start.12 = (f32[32,128]{1,0:T(8,128)}, f32[32,128]{1,0:T(8,128)S(1)}, u32[]{:S(2)}) copy-start(f32[32,128]{1,0:T(8,128)S(1)} %reduce_window_sum.17) | copy-start | bytes 49156
  45.7 13.3 %copy-start.10 = (f32[32,128]{1,0:T(8,128)}, f32[32,128]{1,0:T(8,128)S(1)}, u32[]{:S(2)}) copy-start(f32[32,128]{1,0:T(8,128)S(1)} %reduce_window_sum.18) | copy-start | bytes 49156
  48.7 2.9 copy-start.6
  106.1 1.8 copy-start.8
  106.1 1.8 copy-start.9
  146.2 14.6 %copy-start.2 = (bf16[1664,512]{0,1:T(8,128)(2,1)S(1)}, bf16[1664,512]{0,1:T(8,128)(2,1)}, u32[]{:S(2)}) copy-start(bf16[1664,512]{0,1:T(8,128)(2,1)} %copy.147) | copy-start | bytes 5111812
  174.0 16.0 %copy-start.3 = (bf16[128,4096]{0,1:T(8,128)(2,1)S(1)}, bf16[128,4096]{0,1:T(8,128)(2,1)}, u32[]{:S(2)}) copy-start(bf16[128,4096]{0,1:T(8,128)(2,1)} %copy.201) | copy-start | bytes 3145732
  193.5 17.0 %copy-start = (f32[32,128,128]{2,1,0:T(8,128)}, f32[32,128,128]{2,1,0:T(8,128)S(1)}, u32[]{:S(2)}) copy-start(f32[32,128,128]{2,1,0:T(8,128)S(1)} %fusion.31) | copy-start | bytes 6291460
  193.5 17.0 %copy-start.4 = (bf16[128,4096]{0,1:T(8,128)(2,1)S(1)}, bf16[128,4096]{0,1:T(8,128)(2,1)}, u32[]{:S(2)}) copy-start(bf16[128,4096]{0,1:T(8,128)(2,1)} %copy.204) | copy-start | bytes 3145732
  218.3 3.2 copy-start.19
  255.0 4.6 %copy-start.13 = (f32[32,128]{1,0:T(8,128)S(1)}, f32[32,128]{1,0:T(8,128)}, u32[]{:S(2)}) copy-start(f32[32,128]{1,0:T(8,128)} %copy-done.12) | copy-start | bytes 49156
  259.7 4.8 %copy-start.11 = (f32[32,128]{1,0:T(8,128)S(1)}, f32[32,128]{1,0:T(8,128)}, u32[]{:S(2)}) copy-start(f32[32,128]{1,0:T(8,128)} %copy-done.10) | copy-start | bytes 49156
  382.3 32.0 %copy-start.15 = (f32[128,32]{0,1:T(8,128)S(1)}, f32[128,32]{0,1:T(8,128)}, u32[]{:S(2)}) copy-start(f32[128,32]{0,1:T(8,128)} %get-tuple-element.185) | copy-start | bytes 49156
  414.3 4.0 copy-start.1
  414.3 4.0 copy-start.7
  414.3 4.0 copy-start.14
  414.3 4.0 copy-start.18
Sparse Core Ops, SparseCore 0:
  10.7 77.6 all-gather.5
  215.5 166.7 all-gather.7
where the time goes:
time: 450 us; the launch traced here: 446 us
  waiting for transfers between devices  139 us (31%)
  matrix products  122 us (27%)
  blocking collectives  59.9 us (13%)
  local copies, waits for them, and re-layouts  51.5 us (11%)
  other arithmetic  50.9 us (11%)
  between operations  18.4 us (4%)
    all_gather x1, waiting for transfers between devices, carried_in(): pieces = jax.tree.map(lambda part: lax.all_gather(part, axis), value)  110 us
    dot_general x2, matrix products, attend_block(): jnp.einsum('kgqn,nkd->qkgd', weights, value_part, preferred_element_type=...  33 us
    unnamed x1, blocking collectives  31.9 us
    select_n x15, other arithmetic, turn(): jnp.where(position < mine, new, old)  31.4 us
    dot_general x2, matrix products, attend_block(): jnp.einsum('qkgd,nkd->kgqn', queries, key_part, preferred_element_type=jn...  29 us
    all_gather x1, waiting for transfers between devices, body(): kv_portion = lax.all_gather(kv_local, 'seq', axis=0, tiled=True)  28.8 us
    all_gather x1, blocking collectives, body(): seg_portion = lax.all_gather(segments, 'seq', axis=0, tiled=True)  23.1 us
    sub x2, matrix products, attend_block(): lifted = jnp.exp(scores - highest)  22.1 us
  transfers between devices with their start and end apart: 3, of which 2 were waited for; matrix products, arithmetic and copies ran while one was open for 10% of the time, Pallas kernels for 0%

commit v1 on v0

--- a/solution.py
+++ b/solution.py
@@ -103,7 +103,21 @@
     wanted = jnp.max(jnp.where(owner_match, inner_index[None, :], -1), axis=1)
     wanted_safe = jnp.clip(wanted, 0, block_count - 1)
     owner_table = owner_index.reshape(block_count, block_list.shape[1])
-    kv_portion = lax.all_gather(kv_local, "seq", axis=0, tiled=True)
+    axis_n = lax.axis_size("seq")
+    tray = []
+    for i0 in [*range(axis_n)]:
+        tray.append((i0, (i0 + 1) % axis_n))
+    panels = []
+    for i0 in tuple(range(axis_n)):
+        panels.append((i0, (i0 - 1) % axis_n))
+    outer, u1 = ([kv_local], [kv_local])
+    for _ in range(axis_n // 2):
+        outer.append(lax.ppermute(outer[-1], "seq", tray))
+    for _ in tuple(range((axis_n - 1) // 2)):
+        x_new = lax.ppermute(u1[-1], "seq", panels)
+        u1.append(x_new)
+    inter = jnp.concatenate([*outer[::-1], *u1[1:]], 0)
+    kv_portion = jnp.roll(inter, (lax.axis_index("seq") - axis_n // 2) * kv_local.shape[0], 0)
     seg_portion = lax.all_gather(segments, "seq", axis=0, tiled=True)
     portion_shards = kv_portion.shape[0] // tokens_here
     kv_view = kv_portion.reshape(portion_shards, block_count, BLK, 2 * kv_width)

time: 450 us -> 550 us (1.22)
  local copies, waits for them, and re-layouts: 51.5 us -> 105 us
  starting transfers between devices: 3.38 us -> 56.2 us
  waiting for transfers between devices: 139 us -> 121 us
  blocking collectives: 59.9 us -> 68.8 us
    ppermute x0 -> x15, starting transfers between devices: none -> 53.9 us  [the longest x8 38.2 us: body(): outer.append(lax.ppermute(outer[-1], 'seq', tray))]
    unnamed x51 -> x102, local copies, waits for them, and re-layouts: 13.9 us -> 56.6 us
    all_gather x1 -> x0, waiting for transfers between devices: 28.8 us -> none  [body(): kv_portion = lax.all_gather(kv_local, 'seq', axis=0, tiled=True)]
    unnamed x1, blocking collectives: 31.9 us -> 41.4 us
    ppermute x0 -> x15, waiting for transfers between devices: none -> 8.44 us  [the longest x8 6.37 us: body(): outer.append(lax.ppermute(outer[-1], 'seq', tray))]
    dynamic_slice x0 -> x1, local copies, waits for them, and re-layouts: none -> 7.61 us  [body(): jnp.roll(inter, (lax.axis_index('seq') - axis_n // 2) * kv_local.shape[0]...]
  transfers between devices with their start and end apart: 3 -> 17, of which waited for: 2 -> 6; matrix products, arithmetic and copies ran while one was open for 10% -> 12% of each run, Pallas kernels for 0% -> 0%
where the time goes in v1:
time: 550 us; the launch traced here: 544 us
  matrix products  123 us (22%)
  waiting for transfers between devices  121 us (22%)
  local copies, waits for them, and re-layouts  105 us (19%)
  blocking collectives  68.8 us (13%)
  starting transfers between devices  56.2 us (10%)
  other arithmetic  50.6 us (9%)
  between operations  18.8 us (3%)
    all_gather x1, waiting for transfers between devices, carried_in(): pieces = jax.tree.map(lambda part: lax.all_gather(part, axis), value)  112 us
    unnamed x102, local copies, waits for them, and re-layouts  56.6 us
    unnamed x1, blocking collectives  41.4 us
    ppermute x8, starting transfers between devices, body(): outer.append(lax.ppermute(outer[-1], 'seq', tray))  38.2 us
    dot_general x2, matrix products, attend_block(): jnp.einsum('kgqn,nkd->qkgd', weights, value_part, preferred_element_type=...  33 us
    select_n x15, other arithmetic, turn(): jnp.where(position < mine, new, old)  31.4 us
    dot_general x2, matrix products, attend_block(): jnp.einsum('qkgd,nkd->kgqn', queries, key_part, preferred_element_type=jn...  29.1 us
    all_gather x1, blocking collectives, body(): seg_portion = lax.all_gather(segments, 'seq', axis=0, tiled=True)  22.5 us
  transfers between devices with their start and end apart: 17, of which 6 were waited for; matrix products, arithmetic and copies ran while one was open for 12% of the time, Pallas kernels for 0%

profile of v1, /device:TPU:0, one launch (start us, length us, event | category | flops | bytes accessed | tf_op | source)
XLA Modules:
  0.0 543.7 jit_solution(15432757342246992777)
XLA Ops:
  11.0 5.0 collective-permute-start.8
  25.0 5.4 collective-permute-start.1
  30.5 6.1 %collective-permute-done.1 = bf16[256,1024]{1,0:T(8,128)(2,1)} collective-permute-done((bf16[256,1024]{1,0:T(8,128)(2,1)}, bf16[256,1024]{1,0:T(8,128)(2,1)}, u32[]{:S(2)}, u32[]{:S(2)}) %collective-permute-start.1) | collective-permute-done | bytes 524320 | tf_op jit(solution)/shard_map/ppermute | solution.py:115
  39.3 22.5 %all-gather.2 = s32[16,1,256]{2,1,0:T(1,128)S(1)} all-gather(s32[1,1,256]{2,1,0:T(1,128)S(1)} %bitcast.191), channel_id=1, replica_groups=mesh['seq'=16,'head'=2] {'seq'}, dimensions={0}, use_global_device_ids=true | all-gather | bytes 17408 | tf_op jit(solution)/shard_map/all_gather | solution.py:121
  73.7 4.8 collective-permute-start.4
  80.6 4.6 collective-permute-start.11
  85.3 7.1 %collective-permute-start.5 = (bf16[256,1024]{1,0:T(8,128)(2,1)S(1)}, bf16[256,1024]{1,0:T(8,128)(2,1)S(1)}, u32[]{:S(2)}, u32[]{:S(2)}) collective-permute-start(bf16[256,1024]{1,0:T(8,128)(2,1)S(1)} %collective-permute-done.4), channel_id=1, source_target_pairs={{0,2},{2,4},{4,6},{6,8},{8,10},{10,12},{12,14},{14,16},{16,18},{18... | collective-permute-start | bytes 1572872 | tf_op jit(solution)/shard_map/ppermute | solution.py:115
  96.7 9.8 %collective-permute-start.6 = (bf16[256,1024]{1,0:T(8,128)(2,1)S(1)}, bf16[256,1024]{1,0:T(8,128)(2,1)}, u32[]{:S(2)}, u32[]{:S(2)}) collective-permute-start(bf16[256,1024]{1,0:T(8,128)(2,1)S(1)} %collective-permute-done.5), channel_id=1, source_target_pairs={{0,2},{2,4},{4,6},{6,8},{8,10},{10,12},{12,14},{14,16},{16,18},{18... | collective-permute-start | bytes 1572872 | tf_op jit(solution)/shard_map/ppermute | solution.py:115
  110.9 9.8 %collective-permute-start.7 = (bf16[256,1024]{1,0:T(8,128)(2,1)}, bf16[256,1024]{1,0:T(8,128)(2,1)S(1)}, u32[]{:S(2)}, u32[]{:S(2)}) collective-permute-start(bf16[256,1024]{1,0:T(8,128)(2,1)} %collective-permute-done.6), channel_id=1, source_target_pairs={{0,2},{2,4},{4,6},{6,8},{8,10},{10,12},{12,14},{14,16},{16,18},{18... | collective-permute-start | bytes 1572872 | tf_op jit(solution)/shard_map/ppermute | solution.py:115
  166.9 7.6 %constant_dynamic-slice_fusion = bf16[4096,1024]{1,0:T(8,128)(2,1)} fusion(bf16[8192,1024]{1,0:T(8,128)(2,1)} %constant_dynamic-update-slice_fusion.2, s32[]{:T(128)S(6)} %select_n.77), kind=kLoop, calls=%fused_computation.156 | loop fusion | bytes 16777220 | tf_op jit(solution)/shard_map/jit(_roll_dynamic)/dynamic_slice | solution.py:120
  174.5 14.8 %bitcast_convert_fusion = bf16[2,12,128,1024]{3,1,2,0:T(8,128)(2,1)S(1)} fusion(bf16[16,2,128,1024]{3,2,1,0:T(8,128)(2,1)} %bitcast.160, pred[16,2]{0,1:T(4,128)(4,1)S(1)} %iota_compare_fusion.3, pred[2,12,16]{2,1,0:T(8,128)(4,1)S(1)} %iota_compare_fusion.1), kind=kOutput, calls=%fused_computation.13 | convolution fusion | flops 204473088 | bytes 14680480 | tf_op jit(solution)/shard_map/bkpj,pjnc->bknc/dot_general | solution.py:129
  200.6 14.5 %fusion.85 = f32[4,1664,128,8]{2,1,3,0:T(8,128)} fusion(bf16[1664,4,128,1]{0,2,3,1:T(8,128)(2,1)} %bitcast.165, bf16[128,4,8,128]{0,3,2,1:T(8,128)(2,1)} %bitcast.167), kind=kOutput, calls=%fused_computation.177 | convolution fusion | flops 1744830464 | bytes 30015488 | tf_op jit(solution)/shard_map/qkgd,nkd->kgqn/dot_general | solution.py:46
  215.1 11.3 %fusion.84 = f32[4,8,128]{2,1,0:T(8,128)S(1)} fusion(pred[128,1664]{0,1:T(8,128)(4,1)} %get-tuple-element.160, bf16[1664,4,128,1]{0,2,3,1:T(8,128)(2,1)} %bitcast.166, bf16[128,4,8,128]{0,3,2,1:T(8,128)(2,1)} %bitcast.168), kind=kOutput, calls=%fused_computation.176 | convolution fusion | flops 1772095104 | bytes 2981888 | tf_op jit(solution)/shard_map/sub | solution.py:57
  232.3 14.6 %fusion.86 = f32[4,1664,128,8]{2,1,3,0:T(8,128)} fusion(bf16[1664,4,128,1]{0,2,3,1:T(8,128)(2,1)} %bitcast.163, bf16[128,4,8,128]{0,3,2,1:T(8,128)(2,1)} %bitcast.169), kind=kOutput, calls=%fused_computation.178 | convolution fusion | flops 1744830464 | bytes 30015488 | tf_op jit(solution)/shard_map/qkgd,nkd->kgqn/dot_general | solution.py:46
  246.9 10.8 %fusion.83 = f32[4,8,128]{2,1,0:T(8,128)S(1)} fusion(pred[128,1664]{0,1:T(8,128)(4,1)} %get-tuple-element.161, bf16[1664,4,128,1]{0,2,3,1:T(8,128)(2,1)S(1)} %bitcast.164, bf16[128,4,8,128]{0,3,2,1:T(8,128)(2,1)} %bitcast.170), kind=kOutput, calls=%fused_computation.175 | convolution fusion | flops 1772095104 | bytes 2981888 | tf_op jit(solution)/shard_map/sub | solution.py:57
  260.1 16.0 %fusion.41 = bf16[4,128,8,128]{3,1,2,0:T(8,128)(2,1)} fusion(bf16[1664,4,128,1]{0,2,3,1:T(8,128)(2,1)} %bitcast.186, f32[4,8,128]{2,1,0:T(8,128)S(1)} %fusion.84, f32[4,1664,128,8]{2,1,3,0:T(8,128)} %fusion.85, pred[128,1664]{0,1:T(8,128)(4,1)} %get-tuple-element.160), kind=kOutput, calls=%fused_computation.57 | convolution fusion | flops 1779439232 | bytes 30244864 | tf_op jit(solution)/shard_map/kgqn,nkd->qkgd/dot_general | solution.py:59
  279.7 17.0 %fusion.40 = bf16[4,128,8,128]{3,1,2,0:T(8,128)(2,1)} fusion(bf16[1664,4,128,1]{0,2,3,1:T(8,128)(2,1)} %bitcast.187, f32[4,8,128]{2,1,0:T(8,128)S(1)} %fusion.83, f32[4,1664,128,8]{2,1,3,0:T(8,128)} %fusion.86, pred[128,1664]{0,1:T(8,128)(4,1)} %get-tuple-element.161), kind=kOutput, calls=%fused_computation.56 | convolution fusion | flops 1779439232 | bytes 30244864 | tf_op jit(solution)/shard_map/kgqn,nkd->qkgd/dot_general | solution.py:59
  296.7 4.8 multiply_add_fusion
  309.1 41.4 %all-reduce = f32[512]{0:T(512)S(1)} all-reduce(f32[512]{0:T(512)S(1)} %dynamic-update-slice), channel_id=2, replica_groups=mesh['seq'=16,'head'=2] {'seq'}, use_global_device_ids=true, to_apply=%add | all-reduce | flops 512 | bytes 4096
  355.1 4.9 fusion.42
  367.7 112.2 %all-gather.5.cloned.1.call-done = f32[512,128,128]{2,1,0:T(8,128)} async-done(((f32[32,128,128]{2,1,0:T(8,128)}), f32[512,128,128]{2,1,0:T(8,128)}) %all-gather.5.cloned.1.call-update) | async-done | bytes 33554448 | tf_op jit(solution)/shard_map/all_gather | solution.py:21
  479.9 32.0 %while.14 = (s32[]{:T(128)}, f32[32,128,128]{2,1,0:T(8,128)S(1)}, s32[]{:T(128)}, f32[16,32]{1,0:T(8,128)S(1)}, f32[16,32,128,128]{3,2,1,0:T(8,128)}, /*index=5*/s32[]{:T(128)}, s32[]{:T(128)}) while((s32[]{:T(128)}, f32[32,128,128]{2,1,0:T(8,128)S(1)}, s32[]{:T(128)}, f32[16,32]{1,0:T(8,128)S(1)}, ...), condition=%wide.region_9.10_spmd.clone, body=%wide.region_8.9_spmd.clone.sunk | while | flops 2097156 | bytes 6291945 | solution.py:30
  520.6 5.7 %copy.172 = f32[256,32,128]{0,2,1:T(8,128)} copy(f32[256,32,128]{2,0,1:T(8,128)} %get-tuple-element.141) | data formatting | bytes 8388608 | tf_op jit(solution)/shard_map/concatenate | solution.py:195
  526.2 4.9 psum.7
  (219 shorter events, 168.6 us)
Async XLA Ops:
  7.2 57.3 %copy-start.17 = (f32[32,256]{1,0:T(8,128)S(1)}, f32[32,256]{1,0:T(8,128)}, u32[]{:S(2)}) copy-start(f32[32,256]{1,0:T(8,128)} %param.15) | copy-start | bytes 98308
  7.2 472.7 %all-gather.5.cloned.1.call-start = ((), (), s32[]{:S(2)}) async-start(), calls=%async_computation | async-start | bytes 35651584 | tf_op jit(solution)/shard_map/all_gather | solution.py:21
  10.6 14.4 %collective-permute-start = (bf16[256,1024]{1,0:T(8,128)(2,1)}, bf16[256,1024]{1,0:T(8,128)(2,1)}, u32[]{:S(2)}, u32[]{:S(2)}) collective-permute-start(bf16[256,1024]{1,0:T(8,128)(2,1)} %constant_dynamic-update-slice_fusion), channel_id=1, source_target_pairs={{0,2},{2,4},{4,6},{6,8},{8,10},{10,12},{12,14},{14,16},{16,18},{18... | collective-permute-start | bytes 1572872 | tf_op jit(solution)/shard_map/ppermute | solution.py:115
  11.0 50.8 %collective-permute-start.8 = (bf16[256,1024]{1,0:T(8,128)(2,1)}, bf16[256,1024]{1,0:T(8,128)(2,1)}, u32[]{:S(2)}, u32[]{:S(2)}) collective-permute-start(bf16[256,1024]{1,0:T(8,128)(2,1)} %constant_dynamic-update-slice_fusion), channel_id=1, source_target_pairs={{0,30},{2,0},{4,2},{6,4},{8,6},{10,8},{12,10},{14,12},{16,14},{18,... | collective-permute-start | bytes 1572872 | tf_op jit(solution)/shard_map/ppermute | solution.py:117
  18.1 90.3 %collective-permute-start.15 = (s32[1]{0:T(128)}, s32[1]{0:T(128)}, u32[]{:S(2)}, u32[]{:S(2)}) collective-permute-start(s32[1]{0:T(128)} %add.77), channel_id=1, source_target_pairs={{0,2},{2,4},{4,6},{6,8},{8,10},{10,12},{12,14},{14,16},{16,18},{18... | collective-permute-start | bytes 20 | tf_op jit(solution)/shard_map/ppermute | solution.py:16
  25.0 11.7 %collective-permute-start.1 = (bf16[256,1024]{1,0:T(8,128)(2,1)}, bf16[256,1024]{1,0:T(8,128)(2,1)}, u32[]{:S(2)}, u32[]{:S(2)}) collective-permute-start(bf16[256,1024]{1,0:T(8,128)(2,1)} %collective-permute-done), channel_id=1, source_target_pairs={{0,2},{2,4},{4,6},{6,8},{8,10},{10,12},{12,14},{14,16},{16,18},{18... | collective-permute-start | bytes 1572872 | tf_op jit(solution)/shard_map/ppermute | solution.py:115
  36.7 25.2 %collective-permute-start.2 = (bf16[256,1024]{1,0:T(8,128)(2,1)}, bf16[256,1024]{1,0:T(8,128)(2,1)}, u32[]{:S(2)}, u32[]{:S(2)}) collective-permute-start(bf16[256,1024]{1,0:T(8,128)(2,1)} %collective-permute-done.1), channel_id=1, source_target_pairs={{0,2},{2,4},{4,6},{6,8},{8,10},{10,12},{12,14},{14,16},{16,18},{18... | collective-permute-start | bytes 1572872 | tf_op jit(solution)/shard_map/ppermute | solution.py:115
  61.8 7.4 %collective-permute-start.9 = (bf16[256,1024]{1,0:T(8,128)(2,1)}, bf16[256,1024]{1,0:T(8,128)(2,1)}, u32[]{:S(2)}, u32[]{:S(2)}) collective-permute-start(bf16[256,1024]{1,0:T(8,128)(2,1)} %collective-permute-done.8), channel_id=1, source_target_pairs={{0,30},{2,0},{4,2},{6,4},{8,6},{10,8},{12,10},{14,12},{16,14},{18,... | collective-permute-start | bytes 1572872 | tf_op jit(solution)/shard_map/ppermute | solution.py:117
  61.9 11.8 %collective-permute-start.3 = (bf16[256,1024]{1,0:T(8,128)(2,1)}, bf16[256,1024]{1,0:T(8,128)(2,1)}, u32[]{:S(2)}, u32[]{:S(2)}) collective-permute-start(bf16[256,1024]{1,0:T(8,128)(2,1)} %collective-permute-done.2), channel_id=1, source_target_pairs={{0,2},{2,4},{4,6},{6,8},{8,10},{10,12},{12,14},{14,16},{16,18},{18... | collective-permute-start | bytes 1572872 | tf_op jit(solution)/shard_map/ppermute | solution.py:115
  64.8 67.4 %copy-start.12 = (f32[32,128]{1,0:T(8,128)}, f32[32,128]{1,0:T(8,128)S(1)}, u32[]{:S(2)}) copy-start(f32[32,128]{1,0:T(8,128)S(1)} %reduce_window_sum.17) | copy-start | bytes 49156
  65.1 67.2 %copy-start.10 = (f32[32,128]{1,0:T(8,128)}, f32[32,128]{1,0:T(8,128)S(1)}, u32[]{:S(2)}) copy-start(f32[32,128]{1,0:T(8,128)S(1)} %reduce_window_sum.18) | copy-start | bytes 49156
  66.4 69.6 %copy-start.5 = (bf16[256,512]{1,0:T(8,128)(2,1)S(1)}, bf16[256,512]{1,0:T(8,128)(2,1)}, u32[]{:S(2)}) copy-start(bf16[256,512]{1,0:T(8,128)(2,1)} %param.11) | copy-start | bytes 786436
  67.7 69.0 %copy-start.6 = (bf16[256,512]{1,0:T(8,128)(2,1)S(1)}, bf16[256,512]{1,0:T(8,128)(2,1)}, u32[]{:S(2)}) copy-start(bf16[256,512]{1,0:T(8,128)(2,1)} %param.12) | copy-start | bytes 786436
  69.3 11.3 %collective-permute-start.10 = (bf16[256,1024]{1,0:T(8,128)(2,1)}, bf16[256,1024]{1,0:T(8,128)(2,1)S(1)}, u32[]{:S(2)}, u32[]{:S(2)}) collective-permute-start(bf16[256,1024]{1,0:T(8,128)(2,1)} %collective-permute-done.9), channel_id=1, source_target_pairs={{0,30},{2,0},{4,2},{6,4},{8,6},{10,8},{12,10},{14,12},{16,14},{18,... | collective-permute-start | bytes 1572872 | tf_op jit(solution)/shard_map/ppermute | solution.py:117
  73.7 11.6 %collective-permute-start.4 = (bf16[256,1024]{1,0:T(8,128)(2,1)}, bf16[256,1024]{1,0:T(8,128)(2,1)S(1)}, u32[]{:S(2)}, u32[]{:S(2)}) collective-permute-start(bf16[256,1024]{1,0:T(8,128)(2,1)} %collective-permute-done.3), channel_id=1, source_target_pairs={{0,2},{2,4},{4,6},{6,8},{8,10},{10,12},{12,14},{14,16},{16,18},{18... | collective-permute-start | bytes 1572872 | tf_op jit(solution)/shard_map/ppermute | solution.py:115
  78.5 63.6 %copy-start.19 = (s32[128]{0:T(128)}, s32[128]{0:T(128)S(1)}, u32[]{:S(2)}) copy-start(s32[128]{0:T(128)S(1)} %get-tuple-element.170) | copy-start | bytes 1540
  78.5 63.6 %copy-start.21 = (s32[128]{0:T(128)}, s32[128]{0:T(128)S(1)}, u32[]{:S(2)}) copy-start(s32[128]{0:T(128)S(1)} %get-tuple-element.171) | copy-start | bytes 1540
  80.6 14.5 %collective-permute-start.11 = (bf16[256,1024]{1,0:T(8,128)(2,1)S(1)}, bf16[256,1024]{1,0:T(8,128)(2,1)S(1)}, u32[]{:S(2)}, u32[]{:S(2)}) collective-permute-start(bf16[256,1024]{1,0:T(8,128)(2,1)S(1)} %collective-permute-done.10), channel_id=1, source_target_pairs={{0,30},{2,0},{4,2},{6,4},{8,6},{10,8},{12,10},{14,12},{16,14},{18,... | collective-permute-start | bytes 1572872 | tf_op jit(solution)/shard_map/ppermute | solution.py:117
  85.3 11.4 %collective-permute-start.5 = (bf16[256,1024]{1,0:T(8,128)(2,1)S(1)}, bf16[256,1024]{1,0:T(8,128)(2,1)S(1)}, u32[]{:S(2)}, u32[]{:S(2)}) collective-permute-start(bf16[256,1024]{1,0:T(8,128)(2,1)S(1)} %collective-permute-done.4), channel_id=1, source_target_pairs={{0,2},{2,4},{4,6},{6,8},{8,10},{10,12},{12,14},{14,16},{16,18},{18... | collective-permute-start | bytes 1572872 | tf_op jit(solution)/shard_map/ppermute | solution.py:115
  95.1 15.8 %collective-permute-start.12 = (bf16[256,1024]{1,0:T(8,128)(2,1)S(1)}, bf16[256,1024]{1,0:T(8,128)(2,1)S(1)}, u32[]{:S(2)}, u32[]{:S(2)}) collective-permute-start(bf16[256,1024]{1,0:T(8,128)(2,1)S(1)} %collective-permute-done.11), channel_id=1, source_target_pairs={{0,30},{2,0},{4,2},{6,4},{8,6},{10,8},{12,10},{14,12},{16,14},{18,... | collective-permute-start | bytes 1572872 | tf_op jit(solution)/shard_map/ppermute | solution.py:117
  96.7 14.2 %collective-permute-start.6 = (bf16[256,1024]{1,0:T(8,128)(2,1)S(1)}, bf16[256,1024]{1,0:T(8,128)(2,1)}, u32[]{:S(2)}, u32[]{:S(2)}) collective-permute-start(bf16[256,1024]{1,0:T(8,128)(2,1)S(1)} %collective-permute-done.5), channel_id=1, source_target_pairs={{0,2},{2,4},{4,6},{6,8},{8,10},{10,12},{12,14},{14,16},{16,18},{18... | collective-permute-start | bytes 1572872 | tf_op jit(solution)/shard_map/ppermute | solution.py:115
  110.9 13.0 %collective-permute-start.13 = (bf16[256,1024]{1,0:T(8,128)(2,1)S(1)}, bf16[256,1024]{1,0:T(8,128)(2,1)S(1)}, u32[]{:S(2)}, u32[]{:S(2)}) collective-permute-start(bf16[256,1024]{1,0:T(8,128)(2,1)S(1)} %collective-permute-done.12), channel_id=1, source_target_pairs={{0,30},{2,0},{4,2},{6,4},{8,6},{10,8},{12,10},{14,12},{16,14},{18,... | collective-permute-start | bytes 1572872 | tf_op jit(solution)/shard_map/ppermute | solution.py:117
  110.9 13.2 %collective-permute-start.7 = (bf16[256,1024]{1,0:T(8,128)(2,1)}, bf16[256,1024]{1,0:T(8,128)(2,1)S(1)}, u32[]{:S(2)}, u32[]{:S(2)}) collective-permute-start(bf16[256,1024]{1,0:T(8,128)(2,1)} %collective-permute-done.6), channel_id=1, source_target_pairs={{0,2},{2,4},{4,6},{6,8},{8,10},{10,12},{12,14},{14,16},{16,18},{18... | collective-permute-start | bytes 1572872 | tf_op jit(solution)/shard_map/ppermute | solution.py:115
  123.9 20.6 %collective-permute-start.14 = (bf16[256,1024]{1,0:T(8,128)(2,1)S(1)}, bf16[256,1024]{1,0:T(8,128)(2,1)S(1)}, u32[]{:S(2)}, u32[]{:S(2)}) collective-permute-start(bf16[256,1024]{1,0:T(8,128)(2,1)S(1)} %collective-permute-done.13), channel_id=1, source_target_pairs={{0,30},{2,0},{4,2},{6,4},{8,6},{10,8},{12,10},{14,12},{16,14},{18,... | collective-permute-start | bytes 1572872 | tf_op jit(solution)/shard_map/ppermute | solution.py:117
  (22 other events, 352.8 us)
Sparse Core Ops, SparseCore 0:
  301.7 178.1 all-gather.4
